TPU v7x, 128 devices: a whole 4x4x4 slice. The times are simulated.
128 devices in a mesh: ctx: 16 (over x_hi, z, core), head: 8 (over y, x_lo).
Axes of the slice: x: 4 (x_hi: 2, x_lo: 2; x = x_hi * 2 + x_lo), y: 4, z: 4, core: 2. Of those that a mesh axis runs over, the one named last changes fastest.
Arguments:
- queries: bfloat16 [16384, 32, 128], P('ctx', 'head'), may hold values from -64 to 64
- keys: bfloat16 [16384, 8, 128], P('ctx', 'head'), may hold values from -5 to 5
- values: bfloat16 [16384, 8, 128], P('ctx', 'head'), may hold values from -6 to 6
- grad_out: bfloat16 [16384, 32, 128], P('ctx', 'head'), may hold values from -6 to 6
- doc_lengths: int32 [8], replicated, may hold values from 1 to 4096, 16384 in all
- block_plan: int32 [32], replicated, may hold values from 0 to 31, each once
Outputs:
- attn_out: bfloat16 [16384, 32, 128], P('ctx', 'head')
- grad_queries: bfloat16 [16384, 32, 128], P('ctx', 'head')
- grad_keys: bfloat16 [16384, 8, 128], P('ctx', 'head')
- grad_values: bfloat16 [16384, 8, 128], P('ctx', 'head')
Inputs may be any that keep to these rules, and one draw needn't show every extreme that they name: `block_plan`: a permutation of the 32 position blocks. `doc_lengths`: they sum to 16384; some document has exactly 4096 tokens.
All inputs are finite; a program needn't handle non-finite values.
Results may differ from a plain program's by a relative error of at most 0.025.
Values may be sent and summed in bfloat16 or wider, within the bound.
A program may use at most 128 MiB of HBM per device.

v0:
```python
import math

import jax
import jax.numpy as jnp
from jax import lax
from jax.sharding import PartitionSpec as P

DH = 128
GROUP = 4
BLK = 512


NEG = -1e30


def score_rows(q_rows, k_rows, scale):
    return jnp.einsum("qgd,kd->gqk", q_rows, k_rows, preferred_element_type=jnp.float32) * scale


def grad_core(q_rows, g_rows, row_lse, row_delta, k_rows, v_rows, visible, scale):
    scores = score_rows(q_rows, k_rows, scale)
    probs = jnp.where(visible[None], jnp.exp(scores - row_lse[..., None]), 0.0)
    weights = probs.astype(jnp.bfloat16)
    dprob = jnp.einsum("qgd,kd->gqk", g_rows, v_rows, preferred_element_type=jnp.float32)
    dscore = (probs * (dprob - row_delta[..., None])).astype(jnp.bfloat16)
    return (weights, dscore)


def shards(queries, keys, values, grad_out, doc_lengths, block_plan):
    tok_ctx = queries.shape[0]
    n_ctx = lax.axis_size("ctx")
    total = tok_ctx * n_ctx
    per_dev = tok_ctx // BLK
    scale = 1.0 / math.sqrt(DH)
    rank = lax.axis_index("ctx")
    offsets = jnp.arange(BLK, dtype=jnp.int32)
    row_pos = (block_plan[:, None] * BLK + offsets[None, :]).reshape(total)
    ends = jnp.cumsum(doc_lengths)
    row_doc = jnp.sum((row_pos[:, None] >= ends[None, :]).astype(jnp.int32), axis=1)
    my_pos = lax.dynamic_slice_in_dim(row_pos, rank * tok_ctx, tok_ctx, 0)
    my_doc = lax.dynamic_slice_in_dim(row_doc, rank * tok_ctx, tok_ctx, 0)
    k_all, v_all = (
        lax.all_gather(keys, "ctx", axis=0, tiled=True),
        lax.all_gather(values, "ctx", axis=0, tiled=True),
    )

    def slab_loop(tile, carry, first, count):

        def turn(index, state):
            begin = (first + index) * tok_ctx
            key_pos = lax.dynamic_slice_in_dim(row_pos, begin, tok_ctx, 0)
            key_doc = lax.dynamic_slice_in_dim(row_doc, begin, tok_ctx, 0)
            for block in range(per_dev):
                query_pos = my_pos[block * BLK : (block + 1) * BLK]
                query_doc = my_doc[block * BLK : (block + 1) * BLK]
                visible = (key_doc[None, :] == query_doc[:, None]) & (
                    key_pos[None, :] <= query_pos[:, None]
                )
                live = jnp.any(visible)
                state = lax.cond(
                    live,
                    lambda s, block=block, visible=visible: tile(s, block, begin, index, visible),
                    lambda s: s,
                    state,
                )
            return state

        return lax.fori_loop(0, count, turn, carry)

    q_head = queries
    g_head = grad_out
    k_head = k_all[:, 0, :]
    v_head = v_all[:, 0, :]

    def stats_tile(state, block, begin, index, visible, q_head=q_head, k_head=k_head):
        run_max, run_sum = state
        k_rows = lax.dynamic_slice_in_dim(k_head, begin, tok_ctx, 0)
        scores = score_rows(q_head[block * BLK : (block + 1) * BLK], k_rows, scale)
        masked = jnp.where(visible[None], scores, NEG)
        old = run_max[block]
        new = jnp.maximum(old, jnp.max(masked, axis=-1))
        added = jnp.sum(jnp.where(visible[None], jnp.exp(masked - new[..., None]), 0.0), axis=-1)
        summed = run_sum[block] * jnp.exp(old - new) + added
        return (run_max.at[block].set(new), run_sum.at[block].set(summed))

    empty_stats = jnp.zeros((per_dev, GROUP, BLK), jnp.float32)
    run_max, run_sum = slab_loop(stats_tile, (empty_stats + NEG, empty_stats), 0, n_ctx)
    lse = run_max + jnp.log(run_sum)

    def out_tile(
        acc, block, begin, index, visible, q_head=q_head, k_head=k_head, v_head=v_head, lse=lse
    ):
        k_rows = lax.dynamic_slice_in_dim(k_head, begin, tok_ctx, 0)
        v_rows = lax.dynamic_slice_in_dim(v_head, begin, tok_ctx, 0)
        scores = score_rows(q_head[block * BLK : (block + 1) * BLK], k_rows, scale)
        weights = jnp.where(visible[None], jnp.exp(scores - lse[block][..., None]), 0.0).astype(
            jnp.bfloat16
        )
        return acc.at[block].add(
            jnp.einsum("gqk,kd->gqd", weights, v_rows, preferred_element_type=jnp.float32)
        )

    acc = slab_loop(out_tile, jnp.zeros((per_dev, GROUP, BLK, DH), jnp.float32), 0, n_ctx)
    out_head = acc.astype(jnp.bfloat16)
    g_blocks = jnp.transpose(g_head.reshape(per_dev, BLK, GROUP, DH), (0, 2, 1, 3))
    delta = jnp.sum(out_head.astype(jnp.float32) * g_blocks.astype(jnp.float32), axis=-1)
    out_parts = jnp.transpose(out_head, (0, 2, 1, 3)).reshape(tok_ctx, GROUP, DH)

    def tile_grads(
        block,
        begin,
        visible,
        q_head=q_head,
        g_head=g_head,
        k_head=k_head,
        v_head=v_head,
        lse=lse,
        delta=delta,
    ):
        q_rows = q_head[block * BLK : (block + 1) * BLK]
        g_rows = g_head[block * BLK : (block + 1) * BLK]
        k_rows = lax.dynamic_slice_in_dim(k_head, begin, tok_ctx, 0)
        v_rows = lax.dynamic_slice_in_dim(v_head, begin, tok_ctx, 0)
        weights, dscore = grad_core(
            q_rows, g_rows, lse[block], delta[block], k_rows, v_rows, visible, scale
        )
        return (q_rows, g_rows, k_rows, weights, dscore)

    dq_zero = jnp.zeros((per_dev, GROUP, BLK, DH), jnp.float32)

    def full_tile(state, block, begin, index, visible, tile_grads=tile_grads):
        dq_acc, dk_buf, dv_buf = state
        q_rows, g_rows, k_rows, weights, dscore = tile_grads(block, begin, visible)
        dq_rows = (
            jnp.einsum("gqk,kd->gqd", dscore, k_rows, preferred_element_type=jnp.float32) * scale
        )
        dk_rows = (
            jnp.einsum("gqk,qgd->kd", dscore, q_rows, preferred_element_type=jnp.float32) * scale
        )
        dv_rows = jnp.einsum("gqk,qgd->kd", weights, g_rows, preferred_element_type=jnp.float32)
        dk_buf = lax.dynamic_update_slice_in_dim(
            dk_buf, lax.dynamic_slice_in_dim(dk_buf, begin, tok_ctx, 0) + dk_rows, begin, 0
        )
        dv_buf = lax.dynamic_update_slice_in_dim(
            dv_buf, lax.dynamic_slice_in_dim(dv_buf, begin, tok_ctx, 0) + dv_rows, begin, 0
        )
        return (dq_acc.at[block].add(dq_rows), dk_buf, dv_buf)

    zero_all = jnp.zeros((total, DH), jnp.float32)
    dq_acc, dk_buf, dv_buf = slab_loop(full_tile, (dq_zero, zero_all, zero_all), 0, n_ctx)
    dk_parts = [dk_buf]
    dv_parts = [dv_buf]
    dq_parts = jnp.transpose(dq_acc, (0, 2, 1, 3)).reshape(tok_ctx, GROUP, DH).astype(jnp.bfloat16)
    dk_sum, dv_sum = (
        lax.psum_scatter(jnp.stack(dk_parts, axis=1), "ctx", scatter_dimension=0, tiled=True),
        lax.psum_scatter(jnp.stack(dv_parts, axis=1), "ctx", scatter_dimension=0, tiled=True),
    )
    return (out_parts, dq_parts, dk_sum.astype(jnp.bfloat16), dv_sum.astype(jnp.bfloat16))


def solution(mesh):
    in_specs = (
        P("ctx", "head", None),
        P("ctx", "head", None),
        P("ctx", "head", None),
        P("ctx", "head", None),
        P(),
        P(),
    )
    out_specs = (
        P("ctx", "head", None),
        P("ctx", "head", None),
        P("ctx", "head", None),
        P("ctx", "head", None),
    )
    return jax.shard_map(shards, mesh=mesh, in_specs=in_specs, out_specs=out_specs, check_vma=False)
```

profile of v0, /device:TPU:0, one launch (start us, length us, event | category | flops | bytes accessed | tf_op | source)
XLA Modules:
  0.0 742.4 jit_solution(7161165114657080741)
XLA Ops:
  13.3 54.6 %all-gather.3.cloned.1.call-done = bf16[16384,1,128]{2,0,1:T(8,128)(2,1)} async-done(((bf16[1024,1,128]{2,0,1:T(8,128)(2,1)}), bf16[16384,1,128]{2,0,1:T(8,128)(2,1)}) %all-gather.3.cloned.1.call-update) | async-done | bytes 4194320 | tf_op jit(solution)/shard_map/all_gather | solution.py:43
  67.9 90.1 %while.56 = (s32[]{:T(128)}, f32[2,4,512]{2,1,0:T(4,128)S(1)}, f32[2,4,512]{2,1,0:T(4,128)S(1)}, s32[16384]{0:T(1024)S(1)}, s32[1024]{0:T(1024)S(1)}, /*index=5*...) while((s32[]{:T(128)}, f32[2,4,512]{2,1,0:T(4,128)S(1)}, ...), condition=%wide.region_13.14_spmd, body=%wide.region_2.13_spmd.sunk | while | flops 1111502848 | bytes 38519208 | solution.py:68
  71.1 4.7 conditional.12
  75.9 4.7 conditional.13
  110.2 4.7 conditional.13
  118.2 4.7 conditional.13
  132.7 4.7 conditional.12
  137.4 4.7 conditional.13
  145.4 4.7 conditional.12
  150.1 4.7 conditional.13
  159.6 91.9 %while.57 = (s32[]{:T(128)}, f32[2,4,512,128]{3,2,1,0:T(8,128)}, s32[16384]{0:T(1024)S(1)}, s32[1024]{0:T(1024)S(1)}, s32[16384]{0:T(1024)S(1)}, /*index=5*/s32[...) while((s32[]{:T(128)}, f32[2,4,512,128]{3,2,1,0:T(8,128)}, ...), condition=%wide.region_21.22_spmd, body=%wide.region_14.21_spmd.sunk | while | flops 2168979456 | bytes 8489355 | solution.py:68
  162.6 5.3 conditional.14
  162.7 5.3 fusion.30
  168.0 5.3 conditional.15
  168.0 5.3 fusion.59
  201.2 5.4 conditional.15
  201.2 5.3 fusion.59
  209.6 5.4 conditional.15
  209.6 5.3 fusion.59
  224.2 5.3 conditional.14
  224.2 5.3 fusion.30
  229.5 5.3 conditional.15
  229.5 5.3 fusion.59
  237.8 5.3 conditional.14
  237.8 5.3 fusion.30
  243.1 5.3 conditional.15
  243.1 5.3 fusion.59
  251.5 3.1 fusion.153
  254.8 3.5 broadcast_in_dim.144.clone
  258.3 3.5 broadcast_in_dim.144
  261.7 191.1 %while.58 = (s32[]{:T(128)}, f32[2,4,512,128]{3,2,1,0:T(8,128)S(1)}, f32[16384,128]{1,0:T(8,128)}, f32[16384,128]{1,0:T(8,128)}, s32[16384]{0:T(1024)S(1)}, /*in...) while((s32[]{:T(128)}, ...), condition=%wide.region_30.31_spmd, body=%wide.region_23.30_spmd.sunk | while | flops 5416681472 | bytes 105546448 | solution.py:68
  265.8 15.7 %conditional.16 = ((f32[2,4,512,128]{3,2,1,0:T(8,128)S(1)}, f32[16384,128]{1,0:T(8,128)}, f32[16384,128]{1,0:T(8,128)})) conditional(s32[]{:T(128)} %convert_element_type.155, (f32[2,4,512,128]{3,2,1,0:T(8,128)S(1)}, f32[16384,128]{1,0:T(8,128)}, f32[16384,128]{1,0:T(8,128)}) %tuple.221, (f32[2,4,512,128]{3,2,1,0:T(8,128)S(1)}, ...), branch_computations={%region_26.26_spmd, %region_27.27_spmd} | conditional | flops 2706243584 | bytes 52224144 | solution.py:60
  268.2 4.0 fusion.75
  274.6 3.8 fusion.94
  278.4 3.1 fusion.90
  281.5 15.7 %conditional.17 = ((f32[2,4,512,128]{3,2,1,0:T(8,128)S(1)}, f32[16384,128]{1,0:T(8,128)}, f32[16384,128]{1,0:T(8,128)})) conditional(s32[]{:T(128)} %convert_element_type.154, (f32[2,4,512,128]{3,2,1,0:T(8,128)S(1)}, f32[16384,128]{1,0:T(8,128)}, f32[16384,128]{1,0:T(8,128)}) %get-tuple-element.1529, (f32[2,4,512,128]{3,2,1,0:T(8,128)S(1)}, ...), branch_computations={%region_28.28_spmd, %region_29.29_spmd} | conditional | flops 2706243584 | bytes 52224144 | solution.py:60
  283.8 4.0 fusion.114
  287.9 3.8 fusion.133
  294.0 3.1 fusion.129
  334.3 15.7 %conditional.17 = ((f32[2,4,512,128]{3,2,1,0:T(8,128)S(1)}, f32[16384,128]{1,0:T(8,128)}, f32[16384,128]{1,0:T(8,128)})) conditional(s32[]{:T(128)} %convert_element_type.154, (f32[2,4,512,128]{3,2,1,0:T(8,128)S(1)}, f32[16384,128]{1,0:T(8,128)}, f32[16384,128]{1,0:T(8,128)}) %get-tuple-element.1529, (f32[2,4,512,128]{3,2,1,0:T(8,128)S(1)}, ...), branch_computations={%region_28.28_spmd, %region_29.29_spmd} | conditional | flops 2706243584 | bytes 52224144 | solution.py:60
  336.7 4.0 fusion.114
  340.7 3.8 fusion.133
  346.9 3.1 fusion.129
  354.1 15.7 %conditional.17 = ((f32[2,4,512,128]{3,2,1,0:T(8,128)S(1)}, f32[16384,128]{1,0:T(8,128)}, f32[16384,128]{1,0:T(8,128)})) conditional(s32[]{:T(128)} %convert_element_type.154, (f32[2,4,512,128]{3,2,1,0:T(8,128)S(1)}, f32[16384,128]{1,0:T(8,128)}, f32[16384,128]{1,0:T(8,128)}) %get-tuple-element.1529, (f32[2,4,512,128]{3,2,1,0:T(8,128)S(1)}, ...), branch_computations={%region_28.28_spmd, %region_29.29_spmd} | conditional | flops 2706243584 | bytes 52224144 | solution.py:60
  356.5 4.0 fusion.114
  360.5 3.7 fusion.133
  366.6 3.1 fusion.129
  382.1 15.7 %conditional.16 = ((f32[2,4,512,128]{3,2,1,0:T(8,128)S(1)}, f32[16384,128]{1,0:T(8,128)}, f32[16384,128]{1,0:T(8,128)})) conditional(s32[]{:T(128)} %convert_element_type.155, (f32[2,4,512,128]{3,2,1,0:T(8,128)S(1)}, f32[16384,128]{1,0:T(8,128)}, f32[16384,128]{1,0:T(8,128)}) %tuple.221, (f32[2,4,512,128]{3,2,1,0:T(8,128)S(1)}, ...), branch_computations={%region_26.26_spmd, %region_27.27_spmd} | conditional | flops 2706243584 | bytes 52224144 | solution.py:60
  384.5 4.0 fusion.75
  390.9 3.8 fusion.94
  394.7 3.1 fusion.90
  397.8 15.7 %conditional.17 = ((f32[2,4,512,128]{3,2,1,0:T(8,128)S(1)}, f32[16384,128]{1,0:T(8,128)}, f32[16384,128]{1,0:T(8,128)})) conditional(s32[]{:T(128)} %convert_element_type.154, (f32[2,4,512,128]{3,2,1,0:T(8,128)S(1)}, f32[16384,128]{1,0:T(8,128)}, f32[16384,128]{1,0:T(8,128)}) %get-tuple-element.1529, (f32[2,4,512,128]{3,2,1,0:T(8,128)S(1)}, ...), branch_computations={%region_28.28_spmd, %region_29.29_spmd} | conditional | flops 2706243584 | bytes 52224144 | solution.py:60
  400.1 4.0 fusion.114
  404.1 3.8 fusion.133
  410.3 3.1 fusion.129
  417.5 15.6 %conditional.16 = ((f32[2,4,512,128]{3,2,1,0:T(8,128)S(1)}, f32[16384,128]{1,0:T(8,128)}, f32[16384,128]{1,0:T(8,128)})) conditional(s32[]{:T(128)} %convert_element_type.155, (f32[2,4,512,128]{3,2,1,0:T(8,128)S(1)}, f32[16384,128]{1,0:T(8,128)}, f32[16384,128]{1,0:T(8,128)}) %tuple.221, (f32[2,4,512,128]{3,2,1,0:T(8,128)S(1)}, ...), branch_computations={%region_26.26_spmd, %region_27.27_spmd} | conditional | flops 2706243584 | bytes 52224144 | solution.py:60
  419.9 4.0 fusion.75
  426.3 3.7 fusion.94
  433.1 15.6 %conditional.17 = ((f32[2,4,512,128]{3,2,1,0:T(8,128)S(1)}, f32[16384,128]{1,0:T(8,128)}, f32[16384,128]{1,0:T(8,128)})) conditional(s32[]{:T(128)} %convert_element_type.154, (f32[2,4,512,128]{3,2,1,0:T(8,128)S(1)}, f32[16384,128]{1,0:T(8,128)}, f32[16384,128]{1,0:T(8,128)}) %get-tuple-element.1529, (f32[2,4,512,128]{3,2,1,0:T(8,128)S(1)}, ...), branch_computations={%region_28.28_spmd, %region_29.29_spmd} | conditional | flops 2706243584 | bytes 52224144 | solution.py:60
  435.4 4.0 fusion.114
  439.5 3.7 fusion.133
  445.6 3.1 fusion.129
  457.8 171.1 %reduce-scatter.5.cloned.1.call-done = f32[1024,1,128]{2,0,1:T(8,128)} async-done(((f32[16384,1,128]{2,0,1:T(8,128)}), f32[1024,1,128]{2,0,1:T(8,128)}) %reduce-scatter.5.cloned.1.call-update) | async-done | bytes 524304 | tf_op jit(solution)/shard_map/reduce_scatter | solution.py:156
  630.6 103.5 %reduce-scatter.3.cloned.1.call-done = f32[1024,1,128]{2,0,1:T(8,128)} async-done(((f32[16384,1,128]{2,0,1:T(8,128)}), f32[1024,1,128]{2,0,1:T(8,128)}) %reduce-scatter.3.cloned.1.call-update) | async-done | bytes 524304 | tf_op jit(solution)/shard_map/reduce_scatter | solution.py:155
  (394 shorter events, 197.9 us)
Async XLA Ops:
  7.2 60.8 %all-gather.3.cloned.1.call-start = ((), (), s32[]{:S(2)}) async-start(), calls=%async_computation.2 | async-start | bytes 4456448 | tf_op jit(solution)/shard_map/all_gather | solution.py:43
  7.9 150.2 %all-gather.5.cloned.1.call-start = ((), (), s32[]{:S(2)}) async-start(), calls=%async_computation.3 | async-start | bytes 4456448 | tf_op jit(solution)/shard_map/all_gather | solution.py:44
  8.6 620.2 %reduce-scatter.5.cloned.1.call-start = ((), (), s32[]{:S(2)}) async-start(), calls=%async_computation.5 | async-start | bytes 8912896 | tf_op jit(solution)/shard_map/reduce_scatter | solution.py:156
  13.3 238.2 %copy-start.2 = (bf16[1024,4,128]{2,0,1:T(8,128)(2,1)}, bf16[1024,4,128]{2,0,1:T(8,128)(2,1)S(1)}, u32[]{:S(2)}) copy-start(bf16[1024,4,128]{2,0,1:T(8,128)(2,1)S(1)} %copy.48) | copy-start | bytes 3145732
  265.8 2.4 copy-start.1
  265.8 2.4 copy-start.3
  281.5 2.3 copy-start
  281.5 2.3 copy-start.4
  334.3 2.4 copy-start
  334.3 2.4 copy-start.4
  354.1 2.4 copy-start
  354.1 2.4 copy-start.4
  382.1 2.4 copy-start.1
  382.1 2.4 copy-start.3
  397.8 2.3 copy-start
  397.8 2.3 copy-start.4
  417.5 2.4 copy-start.1
  417.5 2.4 copy-start.3
  433.1 2.3 copy-start
  433.1 2.3 copy-start.4
  452.8 1.2 copy-start.5
  452.8 281.2 %reduce-scatter.3.cloned.1.call-start = ((), (), s32[]{:S(2)}) async-start(), calls=%async_computation.4 | async-start | bytes 8912896 | tf_op jit(solution)/shard_map/reduce_scatter | solution.py:155
Sparse Core Ops, SparseCore 0:
  10.4 57.4 all-gather.2
  70.4 52.7 all-gather.4
  453.0 175.8 reduce-scatter.4
  633.0 101.0 reduce-scatter.2
where the time goes:
time: 746 us; the launch traced here: 742 us
  waiting for transfers between devices  331 us (44%)
  matrix products  187 us (25%)
  other arithmetic  127 us (17%)
  loops' own time  66.2 us (9%)
  local copies, waits for them, and re-layouts  16.7 us (2%)
  between operations  13.9 us (2%)
    reduce_scatter x1, waiting for transfers between devices, shards(): lax.psum_scatter(jnp.stack(dv_parts, axis=1), 'ctx', scatter_dimension=0,...  171 us
    reduce_scatter x1, waiting for transfers between devices, shards(): lax.psum_scatter(jnp.stack(dk_parts, axis=1), 'ctx', scatter_dimension=0,...  103 us
    reduce_or x48, other arithmetic, turn(): live = jnp.any(visible)  101 us
    another operation x3, loops' own time, slab_loop(): return lax.fori_loop(0, count, turn, carry)  64 us
    all_gather x1, waiting for transfers between devices, shards(): lax.all_gather(keys, 'ctx', axis=0, tiled=True)  54.6 us
    dot_general x8, matrix products, out_tile(): jnp.einsum('gqk,kd->gqd', weights, v_rows, preferred_element_type=jnp.flo...  42.5 us
    dot_general x16, matrix products, score_rows(): jnp.einsum('qgd,kd->gqk', q_rows, k_rows, preferred_element_type=jnp.floa...  38.8 us
    dot_general x8, matrix products, grad_core(): jnp.einsum('qgd,kd->gqk', g_rows, v_rows, preferred_element_type=jnp.floa...  32.1 us
  transfers between devices with their start and end apart: 4, of which 3 were waited for; matrix products, arithmetic and copies ran while one was open for 10% of the time, Pallas kernels for 0%

commit v1 on v0

v1 whole, which is shorter than its diff:
```python
import math

import jax
import jax.numpy as jnp
from jax import lax
from jax.experimental import pallas as pl
from jax.experimental.pallas import tpu as pltpu
from jax.sharding import PartitionSpec as P

DH = 128
GROUP = 4
BLK = 512
DOC_MOST = 4096
NDOC = 8
QT = 256
ROWS = QT * GROUP
KT = 256
MAXT = (DOC_MOST + QT) // KT
CH = 256
PER = 1024
NEG = -1e30
SCALE = 1.0 / math.sqrt(DH)
CONST = SCALE * math.log2(math.e)
F32 = jnp.float32
BF16 = jnp.bfloat16


def mm(a, b):
    return jnp.dot(a, b, preferred_element_type=F32)


def attend_kernel(
    rank_ref, len_ref, plan_ref, q_ref, g_ref, kv_ref, o_ref, dq_ref, dkv_ref,
    inv_ref, end_ref, s_ref, p_ref, dkv_acc, qt_ref, gt_ref, gs_ref, m_ref, acc_ref, dqt_ref, stage, sem,
):
    n_blocks = plan_ref.shape[0]
    n_own = kv_ref.shape[0] // (2 * PER)
    rank = rank_ref[0]

    def invert(i, c):
        inv_ref[plan_ref[i]] = i
        return c

    lax.fori_loop(0, n_blocks, invert, 0)
    end_ref[0] = 0
    for d in range(NDOC):
        end_ref[d + 1] = end_ref[d] + len_ref[d]

    def zero(i, c):
        dkv_acc[pl.ds(pl.multiple_of(i * 256, 256), 256), :] = jnp.zeros((256, DH), F32)
        return c

    lax.fori_loop(0, dkv_acc.shape[0] // 256, zero, 0)

    def start_of(position):
        first = jnp.int32(0)
        for d in range(1, NDOC):
            first = jnp.where(position >= end_ref[d], end_ref[d], first)
        return first

    def key_base(kt):
        rb = inv_ref[kt // 2]
        return pl.multiple_of((rb // 2) * (2 * PER) + (rb % 2) * BLK + (kt % 2) * KT, KT)

    def tile(u, c):
        block = u // 2
        pos0 = plan_ref[rank * 2 + block] * BLK + (u % 2) * QT
        rows = pl.ds(pl.multiple_of(u * ROWS, ROWS), ROWS)
        last = pos0 // KT
        first = start_of(pos0) // KT
        full_from = start_of(pos0 + QT - 1)
        count = last - first + 1
        q_pos = pos0 + lax.broadcasted_iota(jnp.int32, (1, ROWS), 1) // GROUP
        q_lo = jnp.zeros((1, ROWS), jnp.int32)
        for d in range(1, NDOC):
            q_lo = jnp.where(q_pos >= end_ref[d], end_ref[d], q_lo)
        qt_ref[...] = q_ref[rows, :].T
        m_ref[...] = jnp.full(m_ref.shape, NEG, F32)
        acc_ref[...] = jnp.zeros(acc_ref.shape, F32)
        dqt_ref[...] = jnp.zeros(dqt_ref.shape, F32)

        def scores(t, c):
            kt = first + t
            k = kv_ref[pl.ds(key_base(kt), KT), :]
            out_rows = pl.ds(pl.multiple_of(t * KT, KT), KT)
            whole = (kt < last) & (kt * KT >= full_from)

            @pl.when(whole)
            def _():
                for c0 in range(0, ROWS, CH):
                    s = mm(k, qt_ref[:, c0 : c0 + CH]) * CONST
                    s_ref[out_rows, c0 : c0 + CH] = s
                    m_ref[:, c0 : c0 + CH] = jnp.maximum(
                        m_ref[:, c0 : c0 + CH], jnp.max(s.reshape(KT // 8, 8, CH), axis=0)
                    )

            @pl.when(jnp.logical_not(whole))
            def _():
                k_pos = kt * KT + lax.broadcasted_iota(jnp.int32, (KT, 1), 0)
                for c0 in range(0, ROWS, CH):
                    s = mm(k, qt_ref[:, c0 : c0 + CH]) * CONST
                    seen = (k_pos >= q_lo[:, c0 : c0 + CH]) & (k_pos <= q_pos[:, c0 : c0 + CH])
                    s = jnp.where(seen, s, NEG)
                    s_ref[out_rows, c0 : c0 + CH] = s
                    m_ref[:, c0 : c0 + CH] = jnp.maximum(
                        m_ref[:, c0 : c0 + CH], jnp.max(s.reshape(KT // 8, 8, CH), axis=0)
                    )

            return c

        lax.fori_loop(0, count, scores, 0)
        top = jnp.max(m_ref[...], axis=0, keepdims=True)
        m_ref[0:1, :] = top

        def outputs(t, c):
            v = kv_ref[pl.ds(key_base(first + t) + PER, KT), :]
            vt = jnp.concatenate([v.T, jnp.ones((16, KT), BF16)], axis=0)
            out_rows = pl.ds(pl.multiple_of(t * KT, KT), KT)
            for c0 in range(0, ROWS, CH):
                p = jnp.exp2(s_ref[out_rows, c0 : c0 + CH] - m_ref[0:1, c0 : c0 + CH]).astype(BF16)
                p_ref[out_rows, c0 : c0 + CH] = p
                acc_ref[:, c0 : c0 + CH] += mm(vt, p)
            return c

        lax.fori_loop(0, count, outputs, 0)
        inv_sum = 1.0 / acc_ref[DH : DH + 1, :]
        out_t = (acc_ref[0:DH, :] * inv_sum).astype(BF16)
        o_ref[rows, :] = out_t.T
        g_t = (g_ref[rows, :].T.astype(F32) * inv_sum).astype(BF16)
        gt_ref[...] = g_t
        gs_ref[...] = g_t.T
        m_ref[1:2, :] = jnp.sum(out_t.astype(F32) * g_t.astype(F32), axis=0, keepdims=True)

        def grads(t, c):
            base = key_base(first + t)
            k = kv_ref[pl.ds(base, KT), :]
            v = kv_ref[pl.ds(base + PER, KT), :]
            kt_ = k.T
            in_rows = pl.ds(pl.multiple_of(t * KT, KT), KT)
            dk = dkv_acc[pl.ds(base, KT), :]
            dv = dkv_acc[pl.ds(base + PER, KT), :]
            for c0 in range(0, ROWS, CH):
                cols = pl.ds(c0, CH)
                p = p_ref[in_rows, cols]
                dv = dv + mm(p, gs_ref[cols, :])
                dp = mm(v, gt_ref[:, cols])
                ds = (p.astype(F32) * (dp - m_ref[1:2, cols])).astype(BF16)
                dk = dk + mm(ds, q_ref[pl.ds(u * ROWS + c0, CH), :])
                dqt_ref[:, cols] += mm(kt_, ds)
            dkv_acc[pl.ds(base, KT), :] = dk
            dkv_acc[pl.ds(base + PER, KT), :] = dv
            return c

        lax.fori_loop(0, count, grads, 0)
        dq_ref[rows, :] = (dqt_ref[...] * SCALE).astype(BF16).T
        return c

    lax.fori_loop(0, q_ref.shape[0] // ROWS, tile, 0)

    def write(i):
        return pltpu.make_async_copy(
            stage.at[i % 2], dkv_ref.at[pl.ds(pl.multiple_of(i * PER, PER), PER), :], sem.at[i % 2]
        )

    def flush(i, c):
        @pl.when(i >= 2)
        def _():
            write(i - 2).wait()

        factor = jnp.where(i % 2 == 0, SCALE, 1.0)
        slot = i % 2
        for r in range(0, PER, 256):
            part = dkv_acc[pl.ds(pl.multiple_of(i * PER + r, 256), 256), :]
            stage[slot, r : r + 256, :] = (part * factor).astype(BF16)
        write(i).start()
        return c

    lax.fori_loop(0, 2 * n_own, flush, 0)
    write(2 * n_own - 2).wait()
    write(2 * n_own - 1).wait()


def attend(rank, doc_lengths, block_plan, q, g, kv):
    n_rows = q.shape[0]
    n_kv = kv.shape[0]
    smem = pl.BlockSpec(memory_space=pltpu.SMEM)
    vmem = pl.BlockSpec(memory_space=pltpu.VMEM)
    return pl.pallas_call(
        attend_kernel,
        out_shape=(
            jax.ShapeDtypeStruct((n_rows, DH), BF16),
            jax.ShapeDtypeStruct((n_rows, DH), BF16),
            jax.ShapeDtypeStruct((n_kv, DH), BF16),
        ),
        in_specs=[smem, smem, smem, vmem, vmem, vmem],
        out_specs=(vmem, vmem, pl.BlockSpec(memory_space=pl.ANY)),
        scratch_shapes=[
            pltpu.SMEM((block_plan.shape[0],), jnp.int32),
            pltpu.SMEM((NDOC + 1,), jnp.int32),
            pltpu.VMEM((MAXT * KT, ROWS), F32),
            pltpu.VMEM((MAXT * KT, ROWS), BF16),
            pltpu.VMEM((n_kv, DH), F32),
            pltpu.VMEM((DH, ROWS), BF16),
            pltpu.VMEM((DH, ROWS), BF16),
            pltpu.VMEM((ROWS, DH), BF16),
            pltpu.VMEM((8, ROWS), F32),
            pltpu.VMEM((DH + 16, ROWS), F32),
            pltpu.VMEM((DH, ROWS), F32),
            pltpu.VMEM((2, PER, DH), BF16),
            pltpu.SemaphoreType.DMA((2,)),
        ],
        compiler_params=pltpu.CompilerParams(vmem_limit_bytes=67043328),
    )(rank, doc_lengths, block_plan, q, g, kv)


MESH = pl.DeviceIdType.MESH
NZ = 4


def place():
    me = lax.axis_index("ctx")
    core = me % 2
    z = (me // 2) % NZ
    x = me // (2 * NZ)

    def at(dx, dz, dc):
        return (((x + dx) % 2) * NZ + (z + dz) % NZ) * 2 + (core + dc) % 2

    return at


def meet(peers):
    barrier = pltpu.get_barrier_semaphore()
    for peer in peers:
        pl.semaphore_signal(barrier, inc=1, device_id={"ctx": peer}, device_id_type=MESH)
    pl.semaphore_wait(barrier, len(peers))


def gather_kernel(k_ref, v_ref, out_ref, own_sem, send_sem, recv_sem):
    at = place()
    me, other, up, down, twin = at(0, 0, 0), at(1, 0, 0), at(0, 1, 0), at(0, NZ - 1, 0), at(0, 0, 1)
    meet((other, up, down, twin))

    def slot(owner, j):
        return out_ref.at[pl.ds(pl.multiple_of((owner * 2 + j) * PER, PER), PER), :]

    sent = []

    def send(owner, j, target, source=None):
        copy = pltpu.make_async_remote_copy(
            src_ref=slot(owner, j) if source is None else source,
            dst_ref=slot(owner, j),
            send_sem=send_sem.at[len(sent)],
            recv_sem=recv_sem.at[owner * 2 + j],
            device_id={"ctx": target},
            device_id_type=MESH,
        )
        copy.start()
        sent.append(copy)

    def arrive(owner, j):
        pltpu.make_async_copy(slot(owner, j), slot(owner, j), recv_sem.at[owner * 2 + j]).wait()

    mine = (k_ref, v_ref)
    for j in (0, 1):
        for target in (other, up, down, twin):
            send(me, j, target, mine[j])
    keep = [pltpu.make_async_copy(mine[j], slot(me, j), own_sem.at[j]) for j in (0, 1)]
    for copy in keep:
        copy.start()

    def relay(dx, dz, j, targets):
        owner = at(dx, dz, 0)
        arrive(owner, j)
        for target in targets:
            send(owner, j, target)

    relay(0, NZ - 1, 0, (up, twin))
    relay(0, 1, 0, (twin,))
    relay(1, 0, 0, (up, down, twin))
    relay(0, 1, 1, (down, twin))
    relay(0, NZ - 1, 1, (twin,))
    relay(1, 0, 1, (up, down, twin))
    relay(0, 2, 0, (twin,))
    relay(0, 2, 1, (twin,))
    relay(1, NZ - 1, 0, (up, twin))
    relay(1, 1, 0, (twin,))
    relay(1, 1, 1, (down, twin))
    relay(1, NZ - 1, 1, (twin,))
    relay(1, 2, 0, (twin,))
    relay(1, 2, 1, (twin,))
    for dx in (0, 1):
        for dz in range(NZ):
            for j in (0, 1):
                arrive(at(dx, dz, 1), j)
    for copy in keep:
        copy.wait()
    for copy in sent:
        copy.wait_send()


def gather(k, v, n_ctx):
    vmem = pl.BlockSpec(memory_space=pltpu.VMEM)
    return pl.pallas_call(
        gather_kernel,
        out_shape=jax.ShapeDtypeStruct((n_ctx * 2 * PER, DH), BF16),
        in_specs=[vmem, vmem],
        out_specs=pl.BlockSpec(memory_space=pl.ANY),
        scratch_shapes=[
            pltpu.SemaphoreType.DMA((2,)),
            pltpu.SemaphoreType.DMA((30,)),
            pltpu.SemaphoreType.DMA((2 * n_ctx,)),
        ],
        compiler_params=pltpu.CompilerParams(collective_id=1, has_side_effects=True),
    )(k, v)


def reduce_kernel(
    part_ref, dk_ref, dv_ref, mine, sib, rel, zin, xin, load_sem, send_sem, sib_sem, rel_sem, zin_sem, xin_sem
):
    at = place()
    other, up, down, twin = at(1, 0, 0), at(0, 1, 0), at(0, NZ - 1, 0), at(0, 0, 1)
    meet((other, up, down, twin))
    sent = []

    def send(source, target_ref, sem, target):
        copy = pltpu.make_async_remote_copy(
            src_ref=source,
            dst_ref=target_ref,
            send_sem=send_sem.at[len(sent)],
            recv_sem=sem,
            device_id={"ctx": target},
            device_id_type=MESH,
        )
        copy.start()
        sent.append(copy)

    def arrive(ref, sem):
        pltpu.make_async_copy(ref, ref, sem).wait()

    def rows_of(owner):
        return part_ref.at[pl.ds(pl.multiple_of(owner * 2 * PER, 2 * PER), 2 * PER), :]

    order = [(1, 2), (0, 2), (1, 1), (1, NZ - 1), (0, 1), (0, NZ - 1), (1, 0), (0, 0)]
    loads = {}
    for n, (dx, dz) in enumerate(order):
        send(rows_of(at(dx, dz, 1)), sib.at[n], sib_sem.at[n], twin)
        loads[n] = pltpu.make_async_copy(rows_of(at(dx, dz, 0)), mine.at[n], load_sem.at[n])
        loads[n].start()
    index = {key: n for n, key in enumerate(order)}

    def add(target, others, count=PER):
        step = 256

        def body(i, c):
            rows = pl.ds(pl.multiple_of(i * step, step), step)
            total = target[rows, :].astype(F32)
            for ref in others:
                total = total + ref[rows, :].astype(F32)
            target[rows, :] = total.astype(BF16)
            return c

        lax.fori_loop(0, count // step, body, 0)

    def pair(dx, dz):
        n = index[(dx, dz)]
        loads[n].wait()
        arrive(sib.at[n], sib_sem.at[n])
        add(mine.at[n], [sib.at[n]], 2 * PER)
        return mine.at[n]

    def half(ref, j):
        return ref.at[pl.ds(j * PER, PER), :]

    for dx in (1, 0):
        total = pair(dx, 2)
        send(half(total, 0), rel.at[dx, 0], rel_sem.at[dx, 0], up)
        send(half(total, 1), rel.at[dx, 1], rel_sem.at[dx, 1], down)
    for dx in (1, 0):
        above = pair(dx, 1)
        send(half(above, 1), half(zin.at[dx, 0], 1), zin_sem.at[dx, 0, 1], up)
        below = pair(dx, NZ - 1)
        send(half(below, 0), half(zin.at[dx, 1], 0), zin_sem.at[dx, 1, 0], down)
        arrive(rel.at[dx, 0], rel_sem.at[dx, 0])
        add(half(above, 0), [rel.at[dx, 0]])
        send(half(above, 0), half(zin.at[dx, 0], 0), zin_sem.at[dx, 0, 0], up)
        arrive(rel.at[dx, 1], rel_sem.at[dx, 1])
        add(half(below, 1), [rel.at[dx, 1]])
        send(half(below, 1), half(zin.at[dx, 1], 1), zin_sem.at[dx, 1, 1], down)
    outs = (dk_ref, dv_ref)
    far = pair(1, 0)
    near = pair(0, 0)
    for j in (1, 0):
        for side in (0, 1):
            arrive(half(zin.at[1, side], j), zin_sem.at[1, side, j])
        add(half(far, j), [half(zin.at[1, 0], j), half(zin.at[1, 1], j)])
        send(half(far, j), half(xin, j), xin_sem.at[j], other)
    for j in (1, 0):
        for side in (0, 1):
            arrive(half(zin.at[0, side], j), zin_sem.at[0, side, j])
    for j in (1, 0):
        arrive(half(xin, j), xin_sem.at[j])

        def body(i, c, j=j):
            rows = pl.ds(pl.multiple_of(i * 256, 256), 256)
            total = half(near, j)[rows, :].astype(F32)
            for ref in (half(zin.at[0, 0], j), half(zin.at[0, 1], j), half(xin, j)):
                total = total + ref[rows, :].astype(F32)
            outs[j][rows, :] = total.astype(BF16)
            return c

        lax.fori_loop(0, PER // 256, body, 0)
    for copy in sent:
        copy.wait_send()


def reduce(part):
    vmem = pl.BlockSpec(memory_space=pltpu.VMEM)
    dma = pltpu.SemaphoreType.DMA
    return pl.pallas_call(
        reduce_kernel,
        out_shape=(jax.ShapeDtypeStruct((PER, DH), BF16),) * 2,
        in_specs=[pl.BlockSpec(memory_space=pl.ANY)],
        out_specs=(vmem, vmem),
        scratch_shapes=[
            pltpu.VMEM((8, 2 * PER, DH), BF16),
            pltpu.VMEM((8, 2 * PER, DH), BF16),
            pltpu.VMEM((2, 2, PER, DH), BF16),
            pltpu.VMEM((2, 2, 2 * PER, DH), BF16),
            pltpu.VMEM((2 * PER, DH), BF16),
            dma((8,)),
            dma((22,)),
            dma((8,)),
            dma((2, 2)),
            dma((2, 2, 2)),
            dma((2,)),
        ],
        compiler_params=pltpu.CompilerParams(
            collective_id=2, has_side_effects=True, vmem_limit_bytes=67043328
        ),
    )(part)


def shards(queries, keys, values, grad_out, doc_lengths, block_plan):
    tok = queries.shape[0]
    n_ctx = lax.axis_size("ctx")
    rank = lax.axis_index("ctx").astype(jnp.int32).reshape(1)
    kv = gather(keys.reshape(tok, DH), values.reshape(tok, DH), n_ctx)
    out, dq, part = attend(
        rank,
        doc_lengths,
        block_plan,
        queries.reshape(tok * GROUP, DH),
        grad_out.reshape(tok * GROUP, DH),
        kv,
    )
    dk, dv = reduce(part)
    return (
        out.reshape(tok, GROUP, DH),
        dq.reshape(tok, GROUP, DH),
        dk.reshape(tok, 1, DH),
        dv.reshape(tok, 1, DH),
    )


def solution(mesh):
    split = P("ctx", "head", None)
    return jax.shard_map(
        shards,
        mesh=mesh,
        in_specs=(split, split, split, split, P(), P()),
        out_specs=(split, split, split, split),
        check_vma=False,
    )
```

time: 746 us -> 192 us (0.26)
  waiting for transfers between devices: 331 us -> 0 us
  matrix products: 187 us -> 0 us
  Pallas kernels: 0 us -> 187 us
  other arithmetic: 127 us -> 0 us
  loops' own time: 66.2 us -> 0 us
  local copies, waits for them, and re-layouts: 16.7 us -> 3.34 us
  between operations: 13.9 us -> 0.66 us
    reduce_scatter x2 -> x0, waiting for transfers between devices: 275 us -> none  [the longest x1 171 us: shards(): lax.psum_scatter(jnp.stack(dv_parts, axis=1), 'ctx', scatter_dimension=0,...]
    dot_general x56 -> x0, matrix products: 187 us -> none  [the longest x8 42.5 us: out_tile(): jnp.einsum('gqk,kd->gqd', weights, v_rows, preferred_element_type=jnp.flo...]
    pallas_call x0 -> x3, Pallas kernels: none -> 187 us  [the longest x1 101 us: attend(): pl.pallas_call(attend_kernel, out_shape=(jax.ShapeDtypeStruct((n_rows, DH...]
    reduce_or x48 -> x0, other arithmetic: 101 us -> none  [turn(): live = jnp.any(visible)]
    another operation x99 -> x0, loops' own time: 66.2 us -> none  [the longest x3 64 us: slab_loop(): return lax.fori_loop(0, count, turn, carry)]
    all_gather x2 -> x0, waiting for transfers between devices: 54.6 us -> none  [the longest x1 54.6 us: shards(): lax.all_gather(keys, 'ctx', axis=0, tiled=True)]
    reduce_sum x10 -> x0, other arithmetic: 20.1 us -> none  [the longest x8 16.8 us: stats_tile(): jnp.sum(jnp.where(visible[None], jnp.exp(masked - new[..., None]), 0.0),...]
  transfers between devices with their start and end apart: 4 -> 0, of which waited for: 3 -> 0; matrix products, arithmetic and copies ran while one was open for 10% -> 0% of each run, Pallas kernels for 0% -> 0%
where the time goes in v1:
time: 192 us; the launch traced here: 191 us
  Pallas kernels  187 us (97%)
  local copies, waits for them, and re-layouts  3.34 us (2%)
    pallas_call x1, Pallas kernels, attend(): pl.pallas_call(attend_kernel, out_shape=(jax.ShapeDtypeStruct((n_rows, DH...  101 us
    pallas_call x1, Pallas kernels, gather(): pl.pallas_call(gather_kernel, out_shape=jax.ShapeDtypeStruct((n_ctx * 2 *...  44.9 us
    pallas_call x1, Pallas kernels, reduce(): pl.pallas_call(reduce_kernel, out_shape=(jax.ShapeDtypeStruct((PER, DH),...  41.1 us

profile of v1, /device:TPU:0, one launch (start us, length us, event | category | flops | bytes accessed | tf_op | source)
XLA Modules:
  0.0 190.8 jit_solution(17539230713380609939)
XLA Ops:
  0.6 44.9 %shard_map.93.kv_ref = bf16[32768,128]{1,0:T(8,128)(2,1)} custom-call(bf16[1024,128]{1,0:T(8,128)(2,1)} %bitcast.11, bf16[1024,128]{1,0:T(8,128)(2,1)} %bitcast.12), custom_call_target="tpu_custom_call" | custom-call | tf_op jit(solution)/shard_map/pallas_call | solution.py:304
  45.6 100.8 %shard_map.94 = (bf16[4096,128]{1,0:T(8,128)(2,1)}, bf16[4096,128]{1,0:T(8,128)(2,1)}, bf16[32768,128]{1,0:T(8,128)(2,1)}) custom-call(s32[1]{0:T(128)} %bitcast.rank_ref, s32[8]{0:T(128)} %len_ref.1, s32[32]{0:T(128)} %plan_ref.1, bf16[4096,128]{1,0:T(8,128)(2,1)} %bitcast.9, bf16[4096,128]{1,0:T(8,128)(2,1)} %bitcast.10, bf16[32768,128]{1,0:T(8,128)(2,1)} %shard_map.93.kv_ref), custom_call_target="tpu_custom_call" | custom-call | tf_op jit(solution)/shard_map/pallas_call | solution.py:188
  146.4 41.1 %shard_map.95 = (bf16[1024,128]{1,0:T(8,128)(2,1)}, bf16[1024,128]{1,0:T(8,128)(2,1)}) custom-call(bf16[32768,128]{1,0:T(8,128)(2,1)} %get-tuple-element.11.part_ref), custom_call_target="tpu_custom_call" | custom-call | tf_op jit(solution)/shard_map/pallas_call | solution.py:420
  187.4 1.7 copy.12
  189.1 1.7 copy.13

commit v2 on v1

v2 whole, which is shorter than its diff:
```python
import math

import jax
import jax.numpy as jnp
from jax import lax
from jax.experimental import pallas as pl
from jax.experimental.pallas import tpu as pltpu
from jax.sharding import PartitionSpec as P

DH = 128
GROUP = 4
BLK = 512
DOC_MOST = 4096
NDOC = 8
QT = 256
ROWS = QT * GROUP
KT = 256
UNROLL = 2
MAXT = (DOC_MOST + QT) // KT
TILES = 4
PER = 1024
NEG = -1e30
SCALE = 1.0 / math.sqrt(DH)
CONST = SCALE * math.log2(math.e)
F32 = jnp.float32
BF16 = jnp.bfloat16


def mm(a, b):
    return jnp.dot(a, b, preferred_element_type=F32)


def attend_kernel(
    rank_ref, len_ref, plan_ref, q_own, g_own, q_lent, g_lent, kv_ref, o_ref, dq_ref, dkv_ref,
    inv_ref, end_ref, first_ref, last_ref, s_ref, p_ref, kv_buf, acc_kv, zeros, q_ref, g_ref,
    qt_ref, gt_ref, gs_ref, m_ref, acc_ref, dqt_ref, load_sem, store_sem, zero_sem, q_sem,
):
    n_blocks = plan_ref.shape[0]
    n_tiles = n_blocks * (BLK // KT)
    rank = rank_ref[0]
    core = rank % 2

    def side_of(u):
        return (u % 2 + core) % 2

    def fetch(u):
        if u < 2:
            rows = pl.ds(pl.multiple_of((u * 2 + side_of(u)) * ROWS, ROWS), ROWS)
            pair = (q_own, g_own)
        else:
            rows = pl.ds((u - 2) * ROWS, ROWS)
            pair = (q_lent, g_lent)
        into = pl.ds(u * ROWS, ROWS)
        return [
            pltpu.make_async_copy(source.at[rows, :], target.at[into, :], q_sem.at[u, a])
            for a, (source, target) in enumerate(zip(pair, (q_ref, g_ref)))
        ]

    fetches = [fetch(u) for u in range(TILES)]
    for copies in fetches:
        for copy in copies:
            copy.start()

    def invert(i, c):
        inv_ref[plan_ref[i]] = i
        return c

    lax.fori_loop(0, n_blocks, invert, 0)
    end_ref[0] = 0
    for d in range(NDOC):
        end_ref[d + 1] = end_ref[d] + len_ref[d]

    def start_of(position):
        first = jnp.int32(0)
        for d in range(1, NDOC):
            first = jnp.where(position >= end_ref[d], end_ref[d], first)
        return first

    def pos_of(u):
        holder = jnp.where(u < 2, rank, rank + 1 - 2 * core)
        return plan_ref[holder * 2 + u % 2] * BLK + side_of(u) * QT

    def home(kt, j):
        rb = inv_ref[kt // 2]
        base = (rb // 2) * (2 * PER) + j * PER + (rb % 2) * BLK + (kt % 2) * KT
        return pl.ds(pl.multiple_of(base, KT), KT)

    def load(kt, j):
        return pltpu.make_async_copy(kv_ref.at[home(kt, j), :], kv_buf.at[kt, j], load_sem.at[kt, j])

    def store(kt, j):
        return pltpu.make_async_copy(kv_buf.at[kt, j], dkv_ref.at[home(kt, j), :], store_sem.at[kt, j])

    def blank(kt, j):
        return pltpu.make_async_copy(zeros, dkv_ref.at[home(kt, j), :], zero_sem)

    def over(u, action, mark=None):
        pos0 = pos_of(u)

        def body(kt, c):
            if mark is None:
                action(kt)
            else:
                pl.when(mark[kt] == u)(lambda: action(kt))
            return c

        lax.fori_loop(start_of(pos0) // KT, pos0 // KT + 1, body, 0)

    def begin(kt):
        for j in (0, 1):
            load(kt, j).start()

    def clear(kt):
        acc_kv[kt] = jnp.zeros((2, KT, DH), F32)

    def ready(kt):
        for j in (0, 1):
            load(kt, j).wait()

    def finish(kt):
        kv_buf[kt, 0] = (acc_kv[kt, 0] * SCALE).astype(BF16)
        kv_buf[kt, 1] = acc_kv[kt, 1].astype(BF16)
        for j in (0, 1):
            store(kt, j).start()

    def stored(kt):
        for j in (0, 1):
            store(kt, j).wait()

    def blanks(act):
        def body(kt, c):
            @pl.when(first_ref[kt] == TILES)
            def _():
                for j in (0, 1):
                    act(blank(kt, j))

            return c

        lax.fori_loop(0, n_tiles, body, 0)

    def unmark(kt, c):
        first_ref[kt] = TILES
        last_ref[kt] = TILES
        return c

    lax.fori_loop(0, n_tiles, unmark, 0)
    for u in range(TILES):

        def mark(kt, u=u):
            last_ref[kt] = u
            first_ref[kt] = jnp.minimum(first_ref[kt], u)

        over(u, mark)
        over(u, begin, first_ref)
    zeros[...] = jnp.zeros(zeros.shape, BF16)
    for u in range(TILES):
        over(u, clear, first_ref)
    blanks(lambda copy: copy.start())

    def tile(u, c):
        pos0 = pos_of(u)
        rows = pl.ds(pl.multiple_of(u * ROWS, ROWS), ROWS)
        last = pos0 // KT
        first = start_of(pos0) // KT
        full_from = start_of(pos0 + QT - 1)
        count = last - first + 1
        q_pos = pos0 + lax.broadcasted_iota(jnp.int32, (1, ROWS), 1) // GROUP
        q_lo = jnp.zeros((1, ROWS), jnp.int32)
        for d in range(1, NDOC):
            q_lo = jnp.where(q_pos >= end_ref[d], end_ref[d], q_lo)
        for a, (source, target) in enumerate(((q_lent, q_ref), (g_lent, g_ref))):
            pltpu.make_async_copy(source.at[pl.ds(0, ROWS), :], target.at[rows, :], q_sem.at[u, a]).wait()
        over(u, ready, first_ref)
        qt_ref[...] = q_ref[rows, :].T
        m_ref[...] = jnp.full(m_ref.shape, NEG, F32)
        acc_ref[...] = jnp.zeros(acc_ref.shape, F32)
        dqt_ref[...] = jnp.zeros(dqt_ref.shape, F32)

        def here(t):
            return pl.ds(pl.multiple_of(t * KT, KT), KT)

        def each(body):
            def run(i, c):
                body(i * UNROLL, UNROLL)
                return c

            lax.fori_loop(0, count // UNROLL, run, 0)
            if UNROLL == 2:
                pl.when(count % 2 == 1)(lambda: body(count - 1, 1))

        def scores(t0, n):
            kt0 = first + t0
            whole = (kt0 + (n - 1) < last) & (kt0 * KT >= full_from)

            def go(masked):
                top = m_ref[...]
                for i in range(n):
                    s = mm(kv_buf[kt0 + i, 0], qt_ref[...]) * CONST
                    if masked:
                        k_pos = (kt0 + i) * KT + lax.broadcasted_iota(jnp.int32, (KT, 1), 0)
                        s = jnp.where((k_pos >= q_lo) & (k_pos <= q_pos), s, NEG)
                    s_ref[here(t0 + i), :] = s
                    top = jnp.maximum(top, jnp.max(s.reshape(KT // 8, 8, ROWS), axis=0))
                m_ref[...] = top

            pl.when(whole)(lambda: go(False))
            pl.when(jnp.logical_not(whole))(lambda: go(True))

        each(scores)
        m_ref[0:1, :] = jnp.max(m_ref[...], axis=0, keepdims=True)

        def outputs(t0, n):
            total = acc_ref[...]
            for i in range(n):
                v = kv_buf[first + t0 + i, 1]
                vt = jnp.concatenate([v.T, jnp.ones((16, KT), BF16)], axis=0)
                p = jnp.exp2(s_ref[here(t0 + i), :] - m_ref[0:1, :]).astype(BF16)
                p_ref[here(t0 + i), :] = p
                total = total + mm(vt, p)
            acc_ref[...] = total

        each(outputs)
        inv_sum = 1.0 / acc_ref[DH : DH + 1, :]
        out_t = (acc_ref[0:DH, :] * inv_sum).astype(BF16)
        o_ref[rows, :] = out_t.T
        g_t = (g_ref[rows, :].T.astype(F32) * inv_sum).astype(BF16)
        gt_ref[...] = g_t
        gs_ref[...] = g_t.T
        m_ref[1:2, :] = jnp.sum(out_t.astype(F32) * g_t.astype(F32), axis=0, keepdims=True)

        def grads(t0, n):
            for i in range(n):
                slot = first + t0 + i
                k = kv_buf[slot, 0]
                p = p_ref[here(t0 + i), :]
                acc_kv[slot, 1] += mm(p, gs_ref[...])
                dp = mm(kv_buf[slot, 1], gt_ref[...])
                ds = (p.astype(F32) * (dp - m_ref[1:2, :])).astype(BF16)
                acc_kv[slot, 0] += mm(ds, q_ref[rows, :])
                dqt_ref[...] += mm(k.T, ds)

        each(grads)
        dq_ref[rows, :] = (dqt_ref[...] * SCALE).astype(BF16).T
        over(u, finish, last_ref)
        return c

    lax.fori_loop(0, TILES, tile, 0)
    blanks(lambda copy: copy.wait())
    for u in range(TILES):
        over(u, stored, last_ref)


def attend(rank, doc_lengths, block_plan, q, g, q_lent, g_lent, kv):
    n_rows = q.shape[0]
    n_kv = kv.shape[0]
    n_tiles = n_kv // (2 * KT)
    smem = pl.BlockSpec(memory_space=pltpu.SMEM)
    vmem = pl.BlockSpec(memory_space=pltpu.VMEM)
    hbm = pl.BlockSpec(memory_space=pl.ANY)
    dma = pltpu.SemaphoreType.DMA
    return pl.pallas_call(
        attend_kernel,
        out_shape=(
            jax.ShapeDtypeStruct((n_rows, DH), BF16),
            jax.ShapeDtypeStruct((n_rows, DH), BF16),
            jax.ShapeDtypeStruct((n_kv, DH), BF16),
        ),
        in_specs=[smem, smem, smem, hbm, hbm, hbm, hbm, hbm],
        out_specs=(vmem, vmem, hbm),
        scratch_shapes=[
            pltpu.SMEM((block_plan.shape[0],), jnp.int32),
            pltpu.SMEM((NDOC + 1,), jnp.int32),
            pltpu.SMEM((n_tiles,), jnp.int32),
            pltpu.SMEM((n_tiles,), jnp.int32),
            pltpu.VMEM((MAXT * KT, ROWS), F32),
            pltpu.VMEM((MAXT * KT, ROWS), BF16),
            pltpu.VMEM((n_tiles, 2, KT, DH), BF16),
            pltpu.VMEM((n_tiles, 2, KT, DH), F32),
            pltpu.VMEM((KT, DH), BF16),
            pltpu.VMEM((TILES * ROWS, DH), BF16),
            pltpu.VMEM((TILES * ROWS, DH), BF16),
            pltpu.VMEM((DH, ROWS), BF16),
            pltpu.VMEM((DH, ROWS), BF16),
            pltpu.VMEM((ROWS, DH), BF16),
            pltpu.VMEM((8, ROWS), F32),
            pltpu.VMEM((DH + 16, ROWS), F32),
            pltpu.VMEM((DH, ROWS), F32),
            dma((n_tiles, 2)),
            dma((n_tiles, 2)),
            dma,
            dma((TILES, 2)),
        ],
        compiler_params=pltpu.CompilerParams(vmem_limit_bytes=67043328),
    )(rank, doc_lengths, block_plan, q, g, q_lent, g_lent, kv)


MESH = pl.DeviceIdType.MESH
NZ = 4
HALF = PER // 2


def place():
    me = lax.axis_index("ctx")
    core = me % 2
    z = (me // 2) % NZ
    x = me // (2 * NZ)

    def at(dx, dz, dc):
        return (((x + dx) % 2) * NZ + (z + dz) % NZ) * 2 + (core + dc) % 2

    return at, core


def meet(peers):
    barrier = pltpu.get_barrier_semaphore()
    for peer in peers:
        pl.semaphore_signal(barrier, inc=1, device_id={"ctx": peer}, device_id_type=MESH)
    pl.semaphore_wait(barrier, len(peers))


def arrive(ref, sem):
    pltpu.make_async_copy(ref, ref, sem).wait()


class Outbox:
    def __init__(self, sems):
        self.sems = sems
        self.copies = []

    def send(self, source, target_ref, sem, target):
        copy = pltpu.make_async_remote_copy(
            src_ref=source,
            dst_ref=target_ref,
            send_sem=self.sems.at[len(self.copies)],
            recv_sem=sem,
            device_id={"ctx": target},
            device_id_type=MESH,
        )
        copy.start()
        self.copies.append(copy)

    def drain(self):
        for copy in self.copies:
            copy.wait_send()


def gather_kernel(
    k_ref, v_ref, q_ref, g_ref, out_ref, qx_ref, gx_ref, own_sem, send_sem, recv_sem, swap_sem
):
    at, core = place()
    me, other, up, down, twin = at(0, 0, 0), at(1, 0, 0), at(0, 1, 0), at(0, NZ - 1, 0), at(0, 0, 1)
    meet((other, up, down, twin))
    box = Outbox(send_sem)

    def slot(owner, j, h):
        return out_ref.at[pl.ds(pl.multiple_of(owner * (2 * PER) + j * PER + h * HALF, HALF), HALF), :]

    def sem(owner, j, h):
        return recv_sem.at[owner * 4 + j * 2 + h]

    def own(j, h):
        return (k_ref, v_ref)[j].at[pl.ds(h * HALF, HALF), :]

    def push(j, h, targets):
        for target in targets:
            box.send(own(j, h), slot(me, j, h), sem(me, j, h), target)

    push(1, 0, (up, down))
    push(0, 0, (other,))
    push(1, 1, (up, down))
    push(0, 1, (other,))
    push(0, 0, (up, down))
    push(1, 0, (other,))
    push(0, 1, (up, down))
    push(1, 1, (other,))
    for i in (0, 1):
        rows = pl.ds(pl.multiple_of((i * 2 + (i + core + 1) % 2) * PER, PER), PER)
        into = pl.ds(i * PER, PER)
        box.send(q_ref.at[rows, :], qx_ref.at[into, :], swap_sem.at[i], twin)
        box.send(g_ref.at[rows, :], gx_ref.at[into, :], swap_sem.at[2 + i], twin)
    keep = []
    for j in (0, 1):
        for h in (0, 1):
            push(j, h, (twin,))
            keep.append(pltpu.make_async_copy(own(j, h), slot(me, j, h), own_sem.at[j * 2 + h]))
            keep[-1].start()

    def relay(dx, dz, j, h, targets):
        owner = at(dx, dz, 0)
        arrive(slot(owner, j, h), sem(owner, j, h))
        for target in targets:
            box.send(slot(owner, j, h), slot(owner, j, h), sem(owner, j, h), target)

    relay(0, 3, 1, 0, (up, other, twin))
    relay(0, 1, 1, 0, (other, twin))
    relay(1, 0, 0, 0, (up, down, twin))
    relay(0, 3, 1, 1, (other, twin))
    relay(0, 1, 1, 1, (down, other, twin))
    relay(1, 0, 0, 1, (up, down, twin))
    relay(0, 3, 0, 0, (up, twin))
    relay(0, 1, 0, 0, (twin,))
    relay(1, 0, 1, 0, (twin,))
    relay(0, 3, 0, 1, (twin,))
    relay(0, 1, 0, 1, (down, twin))
    relay(1, 0, 1, 1, (twin,))
    relay(0, 2, 1, 0, (other, twin))
    relay(0, 2, 1, 1, (other, twin))
    relay(1, 3, 0, 0, (up, twin))
    relay(1, 1, 0, 0, (twin,))
    relay(1, 3, 0, 1, (twin,))
    relay(1, 1, 0, 1, (down, twin))
    for dz in (3, 1):
        for h in (0, 1):
            relay(1, dz, 1, h, (twin,))
    for h in (0, 1):
        relay(0, 2, 0, h, (twin,))
    for h in (0, 1):
        relay(1, 2, 0, h, (twin,))
    for h in (0, 1):
        relay(1, 2, 1, h, (twin,))
    for dx in (0, 1):
        for dz in range(NZ):
            owner = at(dx, dz, 1)
            for j in (0, 1):
                for h in (0, 1):
                    arrive(slot(owner, j, h), sem(owner, j, h))
    for i in (0, 1):
        into = pl.ds(i * PER, PER)
        arrive(qx_ref.at[into, :], swap_sem.at[i])
        arrive(gx_ref.at[into, :], swap_sem.at[2 + i])
    for copy in keep:
        copy.wait()
    box.drain()


def gather(k, v, q, g, n_ctx):
    vmem = pl.BlockSpec(memory_space=pltpu.VMEM)
    hbm = pl.BlockSpec(memory_space=pl.ANY)
    dma = pltpu.SemaphoreType.DMA
    return pl.pallas_call(
        gather_kernel,
        out_shape=(
            jax.ShapeDtypeStruct((n_ctx * 2 * PER, DH), BF16),
            jax.ShapeDtypeStruct((2 * PER, DH), BF16),
            jax.ShapeDtypeStruct((2 * PER, DH), BF16),
        ),
        in_specs=[vmem, vmem, hbm, hbm],
        out_specs=(hbm, hbm, hbm),
        scratch_shapes=[dma((4,)), dma((80,)), dma((4 * n_ctx,)), dma((4,))],
        compiler_params=pltpu.CompilerParams(
            collective_id=1, has_side_effects=True, vmem_limit_bytes=67043328
        ),
    )(k, v, q, g)


ORDER = (
    (1, 1, 2), (0, 1, 2), (1, 1, 1), (0, 1, 1), (0, 1, 3), (1, 1, 3), (0, 0, 2), (1, 1, 0),
    (0, 0, 1), (0, 0, 3), (1, 0, 2), (1, 0, 1), (1, 0, 3), (0, 1, 0), (1, 0, 0), (0, 0, 0),
)


def reduce_kernel(
    part_ref, o_ref, dq_ref, out_ref, gq_ref, dk_ref, dv_ref, mine, sib, rel, zin, xin,
    load_sem, send_sem, sib_sem, rel_sem, zin_sem, xin_sem, swap_sem, keep_sem,
):
    at, core = place()
    other, up, down, twin = at(1, 0, 0), at(0, 1, 0), at(0, NZ - 1, 0), at(0, 0, 1)
    meet((other, up, down, twin))
    box = Outbox(send_sem)

    def rows_of(j, owner):
        return part_ref.at[pl.ds(pl.multiple_of(owner * (2 * PER) + j * PER, PER), PER), :]

    loads = []
    for n, (j, dx, dz) in enumerate(ORDER):
        box.send(rows_of(j, at(dx, dz, 1)), sib.at[n], sib_sem.at[n], twin)
        loads.append(pltpu.make_async_copy(rows_of(j, at(dx, dz, 0)), mine.at[n], load_sem.at[n]))
        loads[n].start()
    keep = []
    for a, (source, target) in enumerate(((o_ref, out_ref), (dq_ref, gq_ref))):
        for i in (0, 1):
            kept = pl.ds(pl.multiple_of((i * 2 + (i + core) % 2) * PER, PER), PER)
            keep.append(
                pltpu.make_async_copy(source.at[pl.ds(i * PER, PER), :], target.at[kept, :], keep_sem.at[a, i])
            )
            keep[-1].start()
            box.send(
                source.at[pl.ds((2 + i) * PER, PER), :], target.at[kept, :], swap_sem.at[a, i], twin
            )

    def total(target, others, count):
        step = 256

        def body(i, c):
            rows = pl.ds(pl.multiple_of(i * step, step), step)
            value = others[0][rows, :].astype(F32)
            for ref in others[1:]:
                value = value + ref[rows, :].astype(F32)
            target[rows, :] = value.astype(BF16)
            return c

        lax.fori_loop(0, count // step, body, 0)

    def half(ref, h):
        return ref.at[pl.ds(h * HALF, HALF), :]

    def pair(j, dx, dz):
        n = ORDER.index((j, dx, dz))
        loads[n].wait()
        arrive(sib.at[n], sib_sem.at[n])
        return mine.at[n], sib.at[n]

    def joined(j, dx, dz, extra=()):
        a, b = pair(j, dx, dz)
        total(a, [a, b, *extra], PER)
        return a

    def across(j, dz):
        arrive(xin.at[dz], xin_sem.at[dz])
        return xin.at[dz]

    def far(cat, piece):
        box.send(half(piece, 0), rel.at[cat, 0], rel_sem.at[cat, 0], up)
        box.send(half(piece, 1), rel.at[cat, 1], rel_sem.at[cat, 1], down)

    def zsend(cat, side, h, piece):
        box.send(half(piece, h), half(zin.at[cat, side], h), zin_sem.at[cat, side, h], (up, down)[side])

    def pass_on(cat, above, below):
        arrive(rel.at[cat, 0], rel_sem.at[cat, 0])
        total(half(above, 0), [half(above, 0), rel.at[cat, 0]], HALF)
        zsend(cat, 0, 0, above)
        arrive(rel.at[cat, 1], rel_sem.at[cat, 1])
        total(half(below, 1), [half(below, 1), rel.at[cat, 1]], HALF)
        zsend(cat, 1, 1, below)

    def sides(cat):
        for h in (1, 0):
            for side in (0, 1):
                arrive(half(zin.at[cat, side], h), zin_sem.at[cat, side, h])
        return [zin.at[cat, 0], zin.at[cat, 1]]

    def cross(dz):
        box.send(joined(1, 1, dz), xin.at[dz], xin_sem.at[dz], other)

    cross(2)
    far(0, joined(0, 1, 2))
    cross(1)
    above = joined(0, 1, 1)
    zsend(0, 0, 1, above)
    below = joined(0, 1, 3)
    zsend(0, 1, 0, below)
    cross(3)
    pass_on(0, above, below)
    far(1, joined(0, 0, 2))
    cross(0)
    above = joined(0, 0, 1)
    zsend(1, 0, 1, above)
    below = joined(0, 0, 3)
    zsend(1, 1, 0, below)
    far(2, joined(1, 0, 2, (across(1, 2),)))
    pass_on(1, above, below)
    above = joined(1, 0, 1, (across(1, 1),))
    zsend(2, 0, 1, above)
    below = joined(1, 0, 3, (across(1, 3),))
    zsend(2, 1, 0, below)
    box.send(joined(0, 1, 0, sides(0)), xin.at[NZ], xin_sem.at[NZ], other)
    pass_on(2, above, below)
    near = pair(1, 0, 0)
    total(dv_ref, [*near, across(1, 0), *sides(2)], PER)
    near = pair(0, 0, 0)
    near = [*near, *sides(1)]
    total(dk_ref, [*near, across(0, NZ)], PER)
    for copy in keep:
        copy.wait()
    for a, target in enumerate((out_ref, gq_ref)):
        for i in (0, 1):
            lent = pl.ds(pl.multiple_of((i * 2 + (i + core + 1) % 2) * PER, PER), PER)
            arrive(target.at[lent, :], swap_sem.at[a, i])
    box.drain()


def reduce(part, o, dq):
    vmem = pl.BlockSpec(memory_space=pltpu.VMEM)
    hbm = pl.BlockSpec(memory_space=pl.ANY)
    dma = pltpu.SemaphoreType.DMA
    small = jax.ShapeDtypeStruct((PER, DH), BF16)
    large = jax.ShapeDtypeStruct(o.shape, BF16)
    return pl.pallas_call(
        reduce_kernel,
        out_shape=(large, large, small, small),
        in_specs=[hbm, hbm, hbm],
        out_specs=(vmem, vmem, vmem, vmem),
        scratch_shapes=[
            pltpu.VMEM((16, PER, DH), BF16),
            pltpu.VMEM((16, PER, DH), BF16),
            pltpu.VMEM((3, 2, HALF, DH), BF16),
            pltpu.VMEM((3, 2, PER, DH), BF16),
            pltpu.VMEM((NZ + 1, PER, DH), BF16),
            dma((16,)),
            dma((43,)),
            dma((16,)),
            dma((3, 2)),
            dma((3, 2, 2)),
            dma((NZ + 1,)),
            dma((2, 2)),
            dma((2, 2)),
        ],
        compiler_params=pltpu.CompilerParams(
            collective_id=2, has_side_effects=True, vmem_limit_bytes=67043328
        ),
    )(part, o, dq)


def shards(queries, keys, values, grad_out, doc_lengths, block_plan):
    tok = queries.shape[0]
    n_ctx = lax.axis_size("ctx")
    rank = lax.axis_index("ctx").astype(jnp.int32).reshape(1)
    q = queries.reshape(tok * GROUP, DH)
    g = grad_out.reshape(tok * GROUP, DH)
    kv, q_lent, g_lent = gather(keys.reshape(tok, DH), values.reshape(tok, DH), q, g, n_ctx)
    out, dq, part = attend(rank, doc_lengths, block_plan, q, g, q_lent, g_lent, kv)
    out, dq, dk, dv = reduce(part, out, dq)
    return (
        out.reshape(tok, GROUP, DH),
        dq.reshape(tok, GROUP, DH),
        dk.reshape(tok, 1, DH),
        dv.reshape(tok, 1, DH),
    )


def solution(mesh):
    split = P("ctx", "head", None)
    return jax.shard_map(
        shards,
        mesh=mesh,
        in_specs=(split, split, split, split, P(), P()),
        out_specs=(split, split, split, split),
        check_vma=False,
    )
```

time: 192 us -> 145 us (0.76); the launches traced: 191 us -> 147 us
  Pallas kernels: 187 us -> 138 us
  local copies, waits for them, and re-layouts: 3.34 us -> 8.45 us
    pallas_call x1, Pallas kernels: 101 us -> 47.2 us  [attend(): pl.pallas_call(attend_kernel, out_shape=(jax.ShapeDtypeStruct((n_rows, DH...]
    unnamed x2 -> x4, local copies, waits for them, and re-layouts: 3.34 us -> 8.45 us
    pallas_call x2, Pallas kernels: 86 us -> 90.5 us  [the longest x1 50.9 us: reduce(): pl.pallas_call(reduce_kernel, out_shape=(large, large, small, small), in_...]
where the time goes in v2:
time: 145 us; the launch traced here: 147 us
  Pallas kernels  138 us (95%)
  local copies, waits for them, and re-layouts  8.45 us (6%)
    pallas_call x1, Pallas kernels, reduce(): pl.pallas_call(reduce_kernel, out_shape=(large, large, small, small), in_...  50.9 us
    pallas_call x1, Pallas kernels, attend(): pl.pallas_call(attend_kernel, out_shape=(jax.ShapeDtypeStruct((n_rows, DH...  47.2 us
    pallas_call x1, Pallas kernels, gather(): pl.pallas_call(gather_kernel, out_shape=(jax.ShapeDtypeStruct((n_ctx * 2...  39.6 us
    unnamed x4, local copies, waits for them, and re-layouts  8.45 us

profile of v2, /device:TPU:0, one launch (start us, length us, event | category | flops | bytes accessed | tf_op | source)
XLA Modules:
  0.0 146.8 jit_solution(11776701049258726906)
XLA Ops:
  0.6 39.6 %shard_map.93 = (bf16[32768,128]{1,0:T(8,128)(2,1)}, bf16[2048,128]{1,0:T(8,128)(2,1)}, bf16[2048,128]{1,0:T(8,128)(2,1)}) custom-call(bf16[1024,128]{1,0:T(8,128)(2,1)} %bitcast.15, bf16[1024,128]{1,0:T(8,128)(2,1)} %bitcast.16, bf16[4096,128]{1,0:T(8,128)(2,1)} %bitcast.9, bf16[4096,128]{1,0:T(8,128)(2,1)} %bitcast.11), custom_call_target="tpu_custom_call" | custom-call | tf_op jit(solution)/shard_map/pallas_call | solution.py:440
  40.2 47.2 %shard_map.94 = (bf16[4096,128]{1,0:T(8,128)(2,1)}, bf16[4096,128]{1,0:T(8,128)(2,1)}, bf16[32768,128]{1,0:T(8,128)(2,1)}) custom-call(s32[1]{0:T(128)} %bitcast.rank_ref, s32[8]{0:T(128)} %len_ref.1, s32[32]{0:T(128)} %plan_ref.1, bf16[4096,128]{1,0:T(8,128)(2,1)} %bitcast.10, bf16[4096,128]{1,0:T(8,128)(2,1)} %bitcast.12, ...), custom_call_target="tpu_custom_call" | custom-call | tf_op jit(solution)/shard_map/pallas_call | solution.py:261
  87.4 50.9 %shard_map.95 = (bf16[4096,128]{1,0:T(8,128)(2,1)}, bf16[4096,128]{1,0:T(8,128)(2,1)}, bf16[1024,128]{1,0:T(8,128)(2,1)}, bf16[1024,128]{1,0:T(8,128)(2,1)}) custom-call(bf16[32768,128]{1,0:T(8,128)(2,1)} %get-tuple-element.17.part_ref, bf16[4096,128]{1,0:T(8,128)(2,1)} %get-tuple-element.18.o_ref, bf16[4096,128]{1,0:T(8,128)(2,1)} %get-tuple-element.19.dq_ref), custom_call_target="tpu_custom_call" | custom-call | tf_op jit(solution)/shard_map/pallas_call | solution.py:589
  138.3 2.6 %copy.14 = bf16[1024,4,128]{2,1,0:T(4,128)(2,1)} copy(bf16[1024,4,128]{2,1,0:T(4,128)(2,1)} %bitcast.14) | data formatting | bytes 2097152
  140.9 2.6 %copy.15 = bf16[1024,4,128]{2,1,0:T(4,128)(2,1)} copy(bf16[1024,4,128]{2,1,0:T(4,128)(2,1)} %bitcast.13) | data formatting | bytes 2097152
  143.4 1.7 %copy.16 = bf16[1024,1,128]{2,0,1:T(8,128)(2,1)} copy(bf16[1024,1,128]{2,0,1:T(8,128)(2,1)} %bitcast.18) | data formatting | bytes 524288
  145.1 1.7 %copy.17 = bf16[1024,1,128]{2,0,1:T(8,128)(2,1)} copy(bf16[1024,1,128]{2,0,1:T(8,128)(2,1)} %bitcast.17) | data formatting | bytes 524288
